TPU v7x, 256 devices: a whole 4x4x8 slice. The times are simulated.
256 devices in a mesh: group: 32 (over y, z), pencil: 8 (over x, core).
Axes of the slice: x: 4, y: 4, z: 8, core: 2. Of those that a mesh axis runs over, the one named last changes fastest.
Arguments:
- mult_iterate: float32 [32, 8, 8192], P('group', 'pencil'), may hold values from -6 to 6
- residual: float32 [32, 8, 8192], P('group', 'pencil'), may hold values from -6 to 6
- direction: float32 [32, 8, 8192], P('group', 'pencil'), may hold values from -6 to 6
- mult_scale: float32 [32, 8, 8192], P('group', 'pencil'), may hold values from 0.5 to 18
- eigen_basis: float32 [128, 3, 64, 64], P('group'), may hold values from -1 to 1
- eigen_values: float32 [128, 3, 64], P('group'), may hold values from 0.2 to 2
- elastic_coef: float32 [128, 3, 3], P('group'), may hold values from 0.5 to 2
- coarse_inverse: float32 [1024, 1024], replicated, may hold values from -1 to 2.5
- send_pos: int32 [32, 8, 16384], P('group', 'pencil'), may hold values from 0 to 24191, as said below
- pair_slots: int32 [32, 8, 2, 8192], P('group', 'pencil'), may hold values from 0 to 16383, as said below
- prim_rows: int32 [32, 8, 32], P('group', 'pencil'), may hold values from 0 to 16383, as said below
- coarse_idx: int32 [32, 8, 32], P('group', 'pencil'), may hold values from 0 to 1023
Outputs:
- new_iterate: float32 [32, 8, 8192], P('group', 'pencil')
- new_residual: float32 [32, 8, 8192], P('group', 'pencil')
- new_direction: float32 [32, 8, 8192], P('group', 'pencil')
Inputs may be any that keep to these rules, and one draw needn't show every extreme that they name: `send_pos`: distinct within each block (g, s). `pair_slots`: in each block (g, s) the two rows together hold every number of 0 to 16383 once. `prim_rows`: distinct within each block (g, s).
All inputs are finite; a program needn't handle non-finite values.
Results may differ from a plain program's by a relative error of at most 0.0003.
Values sent between devices are 32-bit elements; how exact they have to be, the bound alone decides.
No kernel may reach another device: no remote copies, remote signals or barrier semaphores. Data moves between devices by JAX's collectives and lax.ppermute only.
A program may use at most 128 MiB of HBM per device.

v0:
```python
import jax
import jax.numpy as jnp
from jax import lax
from jax.sharding import PartitionSpec as P


def cycle_slot(index, extent):
    cycle_size = 4 * extent - 4
    plane_index = index // cycle_size
    cycle_spot = index % cycle_size
    side_slot = jnp.where(
        cycle_spot < extent,
        cycle_spot,
        jnp.where(
            cycle_spot < 2 * extent - 2,
            cycle_spot + 1,
            jnp.where(cycle_spot < 3 * extent - 4, cycle_spot + 3, cycle_spot + 4),
        ),
    )
    return plane_index * 4 * extent + side_slot


def cycle_to_volume(cycles, extent):
    sides = cycles.reshape(cycles.shape[:-1] + (4, extent))
    count = jnp.arange(extent, dtype=jnp.int32)
    first_edge = (count == 0).astype(jnp.float32)
    last_edge = (count == extent - 1).astype(jnp.float32)
    plane = sides[..., 0, None, :] * first_edge[:, None]
    plane = plane + sides[..., 1, :, None] * first_edge[None, :]
    plane = plane + sides[..., 2, :, None] * last_edge[None, :]
    return plane + sides[..., 3, None, :] * last_edge[:, None]


def volume_to_cycle(volume):
    sides = jnp.stack(
        [volume[..., 0, :], volume[..., :, 0], volume[..., :, -1], volume[..., -1, :]], axis=-2
    )
    return sides.reshape(volume.shape[:-2] + (4 * volume.shape[-1],))


def spectrum(coeffs, along_x, along_y, along_z):
    first = coeffs[None, :, :, 0, None, None] * along_x.T[:, :, None, None, None]
    second = coeffs[None, :, :, 1, None, None] * along_y[None, :, None, :, None]
    third = coeffs[None, :, :, 2, None, None] * along_z[None, :, None, None, :]
    return first + second + third


def forward_yz(volume, basis):
    highest = lax.Precision.HIGHEST
    step_one = jnp.einsum("xpcyz,pzk->xpcyk", volume, basis[:, 2], precision=highest)
    return jnp.einsum("xpcyk,pyj->xpcjk", step_one, basis[:, 1], precision=highest)


def backward_yz(volume, basis):
    highest = lax.Precision.HIGHEST
    step_one = jnp.einsum("xpcjk,pyj->xpcyk", volume, basis[:, 1], precision=highest)
    return jnp.einsum("xpcyk,pzk->xpcyz", step_one, basis[:, 2], precision=highest)


def load_slab(arrived_rows, positions, slab_shape):
    cycle_total = slab_shape[0] * slab_shape[1] * slab_shape[2] * 4 * slab_shape[3]
    cycles = jnp.zeros((cycle_total,), jnp.float32).at[positions].set(arrived_rows)
    cycles = cycles.reshape(slab_shape[0], slab_shape[1], slab_shape[2], 4 * slab_shape[3])
    return cycle_to_volume(cycles, slab_shape[3])


def apply_inverse(arrived_rows, cycle_cells, basis, values, coeffs):
    highest = lax.Precision.HIGHEST
    pencils = lax.axis_size("pencil")
    extent = basis.shape[-1]
    patches = basis.shape[0]
    components = coeffs.shape[1]
    slab_x = extent // pencils
    slab_shape = (slab_x, patches, components, extent, extent)
    my_slab = lax.axis_index("pencil")
    row_start = my_slab * slab_x
    positions = cycle_slot(cycle_cells, extent)
    partial_yz = forward_yz(load_slab(arrived_rows, positions, slab_shape), basis)
    columns = lax.all_to_all(
        partial_yz.reshape(slab_x, patches, components, extent * extent),
        "pencil",
        split_axis=3,
        concat_axis=0,
        tiled=True,
    )
    columns = columns.reshape(extent, patches, components, slab_x, extent)
    spectral = jnp.einsum("xpcjk,pxi->ipcjk", columns, basis[:, 0], precision=highest)
    along_y = lax.dynamic_slice_in_dim(values[:, 1], row_start, slab_x, 1)
    scaled = spectral / spectrum(coeffs, values[:, 0], along_y, values[:, 2])
    mixed = jnp.einsum("ipcjk,pxi->xpcjk", scaled, basis[:, 0], precision=highest)
    mixed = mixed.reshape(extent, patches, components, slab_x * extent)
    back_x = lax.all_to_all(mixed, "pencil", split_axis=0, concat_axis=3, tiled=True).reshape(
        slab_shape
    )
    displace = backward_yz(back_x, basis)
    return volume_to_cycle(displace).reshape(-1)[positions]


def body(
    mult_iterate,
    residual,
    direction,
    mult_scale,
    eigen_basis,
    eigen_values,
    elastic_coef,
    coarse_inverse,
    send_pos,
    pair_slots,
    prim_rows,
    coarse_idx,
):
    highest = lax.Precision.HIGHEST
    groups = lax.axis_size("group")
    iterate_now = mult_iterate[0, 0]
    resid_now = residual[0, 0]
    search_dir = direction[0, 0]
    scale_now = mult_scale[0, 0]
    pair_rows = pair_slots[0, 0]
    cycle_cells = send_pos[0, 0]
    primal = prim_rows[0, 0]
    coarse_ids = coarse_idx[0, 0]
    rows_count = cycle_cells.shape[0]
    per_owner = rows_count // groups
    coarse_count = coarse_inverse.shape[0]
    old_part = jnp.sum(resid_now * scale_now * resid_now)
    old_norm = lax.psum(old_part, ("group", "pencil"))
    back_rows = (
        jnp.zeros((rows_count,), jnp.float32)
        .at[pair_rows[0]]
        .set(search_dir)
        .at[pair_rows[1]]
        .set(-search_dir)
    )
    arrived_rows = lax.all_to_all(
        back_rows.reshape(groups, per_owner), "group", split_axis=0, concat_axis=0, tiled=True
    ).reshape(rows_count)
    picked = apply_inverse(arrived_rows, cycle_cells, eigen_basis, eigen_values, elastic_coef)
    onehot = (coarse_ids[:, None] == jnp.arange(coarse_count, dtype=jnp.int32)[None, :]).astype(
        jnp.float32
    )
    local_coarse = jnp.dot(picked[primal], onehot, precision=highest)
    total_coarse = lax.psum(local_coarse, ("group", "pencil"))
    lifted = jnp.dot(coarse_inverse, total_coarse, precision=highest)
    sent_rows = picked.at[primal].add(jnp.dot(onehot, lifted, precision=highest))
    owner_rows = lax.all_to_all(
        sent_rows.reshape(groups, per_owner), "group", split_axis=0, concat_axis=0, tiled=True
    ).reshape(rows_count)
    mapped = owner_rows[pair_rows[0]] - owner_rows[pair_rows[1]]
    curvature = lax.psum(jnp.sum(search_dir * mapped), ("group", "pencil"))
    step_size = old_norm / curvature
    iterate_next = iterate_now + step_size * search_dir
    resid_next = resid_now - step_size * mapped
    precond = scale_now * resid_next
    norm_next = lax.psum(jnp.sum(resid_next * precond), ("group", "pencil"))
    search_next = precond + norm_next / old_norm * search_dir
    return (iterate_next[None, None], resid_next[None, None], search_next[None, None])


def solution(mesh):
    in_specs = (
        P("group", "pencil", None),
        P("group", "pencil", None),
        P("group", "pencil", None),
        P("group", "pencil", None),
        P("group", None, None, None),
        P("group", None, None),
        P("group", None, None),
        P(),
        P("group", "pencil", None),
        P("group", "pencil", None, None),
        P("group", "pencil", None),
        P("group", "pencil", None),
    )
    out_specs = (P("group", "pencil", None), P("group", "pencil", None), P("group", "pencil", None))
    return jax.shard_map(body, mesh=mesh, in_specs=in_specs, out_specs=out_specs, check_vma=False)
```

profile of v0, /device:TPU:1, one launch (start us, length us, event | category | flops | bytes accessed | tf_op | source)
XLA Modules:
  0.0 876.2 jit_solution(14388846261782737221)
XLA Ops:
  0.6 1.0 compare_select_fusion.4
  1.7 0.8 neg.3
  2.4 31.2 %scatter_custom_fusion = f32[16384]{0:T(1024)} fusion(s32[8192]{0:T(1024)S(1)} %bitcast.164, f32[8192]{0:T(1024)} %bitcast.154, f32[]{:T(128)} %constant.16.clone.1), kind=kCustom, calls=%fused_computation.81 | custom fusion | bytes 66048 | tf_op jit(solution)/shard_map/scatter | solution.py:131
  33.7 31.9 %scatter_fusion = f32[16384]{0:T(1024)} fusion(f32[16384]{0:T(1024)} %scatter_custom_fusion, s32[8192]{0:T(1024)S(1)} %bitcast.151, f32[8192]{0:T(1024)S(1)} %neg.3), kind=kCustom, calls=%fused_computation.5 | custom fusion | bytes 131072 | tf_op jit(solution)/shard_map/scatter | solution.py:133
  65.6 12.0 %all-to-all-start = ((f32[32,1,512]{2,1,0:T(1,128)}), f32[32,1,512]{2,1,0:T(1,128)S(1)}, u32[]{:S(2)}, u32[]{:S(2)}) async-start(f32[32,1,512]{2,1,0:T(1,128)} %bitcast.11), calls=%async_computation | async-start | bytes 131072 | tf_op jit(solution)/shard_map/all_to_all | solution.py:135
  77.6 0.8 compare_select_fusion
  78.5 8.0 all-to-all-done
  86.5 60.8 %scatter_custom_fusion.2 = f32[24576]{0:T(1024)S(1)} fusion(s32[16384]{0:T(1024)S(1)} %bitcast.160, f32[16384]{0:T(1024)S(1)} %bitcast.167, f32[]{:T(128)} %constant.16.clone.1), kind=kCustom, calls=%fused_computation.72 | custom fusion | bytes 98308 | tf_op jit(solution)/shard_map/scatter | solution.py:62
  147.3 0.1 reshape_reshape.6
  147.4 0.1 fusion.59
  147.7 4.0 fusion.8
  151.7 5.2 fusion.16
  156.9 34.6 %copy.135 = f32[8,4,3,64,64]{0,1,2,4,3:T(4,128)} copy(f32[8,4,3,64,64]{3,4,2,0,1:T(8,128)S(1)} %fusion.16) | data formatting | bytes 3145728 | tf_op jit(solution)/shard_map/reshape | solution.py:80
  191.5 31.9 %reshape.387 = f32[8,1,49152]{2,1,0:T(1,128)} reshape(f32[4096,3,4,8]{3,2,1,0:T(4,128)} %bitcast.146) | data formatting | bytes 3145728
  223.4 6.5 all-to-all-start.1
  229.9 0.1 fusion.60
  230.0 0.1 copy.117
  230.1 0.1 copy.116
  230.2 0.1 copy.118
  230.3 0.1 dynamic-slice_bitcast_fusion
  230.4 0.1 broadcast_multiply_fusion.2
  230.5 0.1 broadcast_multiply_fusion.3
  230.6 0.1 broadcast_multiply_fusion.1
  230.6 0.7 broadcast_add_fusion
  231.3 19.2 %all-to-all-done.1 = f32[8,1,49152]{2,1,0:T(1,128)S(1)} async-done(((f32[8,1,49152]{2,1,0:T(1,128)}), f32[8,1,49152]{2,1,0:T(1,128)S(1)}, u32[]{:S(2)}, u32[]{:S(2)}) %all-to-all-start.1) | async-done | bytes 1572896 | tf_op jit(solution)/shard_map/all_to_all | solution.py:79
  250.5 0.5 broadcast.300
  251.0 4.4 reduce
  255.4 38.7 %reshape.388 = f32[4096,3,4,8]{3,2,1,0:T(4,128)} reshape(f32[8,49152]{1,0:T(8,128)S(1)} %reduce) | data formatting | bytes 3145728
  294.1 20.7 %copy.137 = f32[8,4,3,8,512]{4,0,3,2,1:T(8,128)} copy(f32[8,4,3,8,512]{0,1,2,4,3:T(4,128)} %bitcast.147) | data formatting | bytes 3145728 | tf_op jit(solution)/shard_map/all_to_all | solution.py:79
  314.8 2.6 reshape.305
  317.4 5.1 fusion.5
  322.5 3.2 fusion.2
  325.8 2.1 copy.119
  327.8 4.6 all-to-all-start.2
  332.5 0.6 broadcast_clamp_fusion.1
  333.1 0.6 broadcast_clamp_fusion
  333.7 19.3 %all-to-all-done.2 = f32[64,4,3,512]{3,1,2,0:T(4,128)S(1)} async-done(((f32[64,4,3,512]{3,1,2,0:T(4,128)}), f32[64,4,3,512]{3,1,2,0:T(4,128)S(1)}, u32[]{:S(2)}, u32[]{:S(2)}) %all-to-all-start.2) | async-done | bytes 1572896 | tf_op jit(solution)/shard_map/all_to_all | solution.py:92
  353.0 0.5 copy.152
  353.5 2.1 copy.140
  355.6 2.6 reshape.382
  358.3 5.1 fusion.35
  363.4 5.1 fusion.19
  368.5 2.7 fusion.58
  371.3 2.5 copy.124
  373.9 1.5 copy.125
  375.5 0.2 pad_maximum_fusion
  375.8 0.1 reshape_reshape.7
  375.9 160.4 %gather_fusion = f32[16384]{0:T(1024)} fusion(f32[24576]{0:T(1024)S(1)} %reshape_reshape.7, s32[16384]{0:T(1024)S(1)} %copy-done.8), kind=kCustom, calls=%fused_computation | custom fusion | bytes 196608 | tf_op jit(solution)/shard_map/gather | solution.py:96
  536.3 1.6 gather_fusion.1
  537.9 0.2 fusion.40
  538.1 72.8 %psum.29 = f32[1024]{0:T(1024)S(1)} all-reduce(f32[1024]{0:T(1024)S(1)} %bitcast.172), channel_id=1, replica_groups=mesh['group'=32,'pencil'=8] {'group','pencil'}, use_global_device_ids=true, to_apply=%region_5.6 | all-reduce | flops 1024 | bytes 8192 | tf_op jit(solution)/shard_map/psum | solution.py:143
  610.9 5.6 convolution_bitcast_fusion
  616.6 0.2 convolution_bitcast_fusion.1
  616.8 2.2 scatter_fusion.1
  619.0 5.0 all-to-all-start.3
  624.1 0.6 fusion.51
  624.7 8.2 all-to-all-done.3
  632.9 45.5 %gather_fusion.3 = f32[8192]{0:T(1024)S(1)} fusion(f32[16384]{0:T(1024)S(1)} %bitcast.144, s32[8192]{0:T(1024)S(1)} %copy-done.11), kind=kCustom, calls=%fused_computation.3 | custom fusion | bytes 98304 | tf_op jit(solution)/shard_map/gather | solution.py:149
  678.5 45.5 %gather_fusion.2 = f32[8192]{0:T(1024)S(1)} fusion(f32[16384]{0:T(1024)S(1)} %bitcast.145, s32[8192]{0:T(1024)S(1)} %broadcast_clamp_fusion.2), kind=kCustom, calls=%fused_computation.2 | custom fusion | bytes 98304 | tf_op jit(solution)/shard_map/gather | solution.py:149
  724.0 0.6 multiply_reduce_fusion
  724.6 73.3 %all-reduce = (f32[]{:T(128)}, f32[]{:T(128)}) all-reduce(f32[]{:T(128)} %fusion.51, f32[]{:T(128)} %get-tuple-element.9), channel_id=1, replica_groups=mesh['group'=32,'pencil'=8] {'group','pencil'}, use_global_device_ids=true, to_apply=%region_1.0 | all-reduce | flops 2 | bytes 16 | tf_op jit(solution)/shard_map/psum | solution.py:127
  799.3 0.6 fusion.52
  799.9 74.0 %psum.31 = f32[]{:T(128)} all-reduce(f32[]{:T(128)} %get-tuple-element.7), channel_id=1, replica_groups=mesh['group'=32,'pencil'=8] {'group','pencil'}, use_global_device_ids=true, to_apply=%region_10.11 | all-reduce | flops 1 | bytes 8 | tf_op jit(solution)/shard_map/psum | solution.py:155
  875.3 0.7 multiply_add_fusion
  (53 shorter events, 0.4 us)
Async XLA Ops:
  1.6 64.0 %copy-start.1 = (s32[8192,1]{0,1:T(1,128)}, s32[8192,1]{0,1:T(1,128)S(1)}, u32[]{:S(2)}) copy-start(s32[8192,1]{0,1:T(1,128)S(1)} %get-tuple-element.19) | copy-start | bytes 98308
  1.6 63.9 %copy-start.9 = (s32[8192,1]{0,1:T(1,128)}, s32[8192,1]{0,1:T(1,128)S(1)}, u32[]{:S(2)}) copy-start(s32[8192,1]{0,1:T(1,128)S(1)} %get-tuple-element.20) | copy-start | bytes 98308
  33.7 44.0 %copy-start.12 = (s32[1,1,16384]{2,1,0:T(1,128)S(1)}, s32[1,1,16384]{2,1,0:T(1,128)}, u32[]{:S(2)}) copy-start(s32[1,1,16384]{2,1,0:T(1,128)} %param.20) | copy-start | bytes 196612
  33.7 114.0 %copy-start = (f32[4,3,64,64]{3,2,1,0:T(8,128)S(1)}, f32[4,3,64,64]{3,2,1,0:T(8,128)}, u32[]{:S(2)}) copy-start(f32[4,3,64,64]{3,2,1,0:T(8,128)} %param.16) | copy-start | bytes 589828
  65.6 20.9 %all-to-all-start = ((f32[32,1,512]{2,1,0:T(1,128)}), f32[32,1,512]{2,1,0:T(1,128)S(1)}, u32[]{:S(2)}, u32[]{:S(2)}) async-start(f32[32,1,512]{2,1,0:T(1,128)} %bitcast.11), calls=%async_computation | async-start | bytes 131072 | tf_op jit(solution)/shard_map/all_to_all | solution.py:135
  78.4 8.1 copy-start.6
  223.4 6.5 copy-start.13
  223.4 7.0 copy-start.16
  223.4 27.1 %all-to-all-start.1 = ((f32[8,1,49152]{2,1,0:T(1,128)}), f32[8,1,49152]{2,1,0:T(1,128)S(1)}, u32[]{:S(2)}, u32[]{:S(2)}) async-start(f32[8,1,49152]{2,1,0:T(1,128)} %reshape.387), calls=%async_computation.1 | async-start | bytes 3145728 | tf_op jit(solution)/shard_map/all_to_all | solution.py:79
  317.4 5.1 copy-start.14
  325.8 6.7 copy-start.17
  327.8 4.6 copy-start.2
  327.8 5.2 copy-start.7
  327.8 25.2 %all-to-all-start.2 = ((f32[64,4,3,512]{3,1,2,0:T(4,128)}), f32[64,4,3,512]{3,1,2,0:T(4,128)S(1)}, u32[]{:S(2)}, u32[]{:S(2)}) async-start(f32[64,4,3,512]{3,1,2,0:T(4,128)} %copy.119), calls=%async_computation.2 | async-start | bytes 3145728 | tf_op jit(solution)/shard_map/all_to_all | solution.py:92
  371.3 4.6 copy-start.8
  375.9 162.0 %copy-start.18 = (s32[1,1,32]{2,1,0:T(1,128)S(1)}, s32[1,1,32]{2,1,0:T(1,128)}, u32[]{:S(2)}) copy-start(s32[1,1,32]{2,1,0:T(1,128)} %param.23) | copy-start | bytes 388
  536.3 87.7 %copy-start.10 = (s32[8192,1]{0,1:T(1,128)S(1)}, s32[8192,1]{0,1:T(1,128)}, u32[]{:S(2)}) copy-start(s32[8192,1]{0,1:T(1,128)} %copy-done.9) | copy-start | bytes 98308
  536.3 87.7 %copy-start.4 = (f32[1,1,8192]{2,1,0:T(1,128)S(1)}, f32[1,1,8192]{2,1,0:T(1,128)}, u32[]{:S(2)}) copy-start(f32[1,1,8192]{2,1,0:T(1,128)} %param.15) | copy-start | bytes 98308
  536.3 87.7 %copy-start.5 = (f32[1,1,8192]{2,1,0:T(1,128)S(1)}, f32[1,1,8192]{2,1,0:T(1,128)}, u32[]{:S(2)}) copy-start(f32[1,1,8192]{2,1,0:T(1,128)} %param.13) | copy-start | bytes 98308
  536.3 96.6 %copy-start.11 = (s32[8192]{0:T(1024)S(1)}, s32[8192]{0:T(1024)}, u32[]{:S(2)}) copy-start(s32[8192]{0:T(1024)} %broadcast_clamp_fusion.1) | copy-start | bytes 98308
  619.0 13.9 %all-to-all-start.3 = ((f32[32,1,512]{2,1,0:T(1,128)}), f32[32,1,512]{2,1,0:T(1,128)S(1)}, u32[]{:S(2)}, u32[]{:S(2)}) async-start(f32[32,1,512]{2,1,0:T(1,128)} %bitcast.57), calls=%async_computation.3 | async-start | bytes 131072 | tf_op jit(solution)/shard_map/all_to_all | solution.py:146
  678.4 45.6 %copy-start.3 = (f32[1,1,8192]{2,1,0:T(1,128)S(1)}, f32[1,1,8192]{2,1,0:T(1,128)}, u32[]{:S(2)}) copy-start(f32[1,1,8192]{2,1,0:T(1,128)} %param.14) | copy-start | bytes 98308
  678.4 196.8 %copy-start.15 = (f32[1,1,8192]{2,1,0:T(1,128)S(1)}, f32[1,1,8192]{2,1,0:T(1,128)}, u32[]{:S(2)}) copy-start(f32[1,1,8192]{2,1,0:T(1,128)} %param.12) | copy-start | bytes 98308
where the time goes:
time: 881 us; the launch traced here: 876 us
  local copies, waits for them, and re-layouts  521 us (59%)
  blocking collectives  220 us (25%)
  waiting for transfers between devices  54.7 us (6%)
  matrix products  33.9 us (4%)
  starting transfers between devices  28.2 us (3%)
  other arithmetic  14.1 us (2%)
    gather x1, local copies, waits for them, and re-layouts, apply_inverse(): return volume_to_cycle(displace).reshape(-1)[positions]  160 us
    gather x2, local copies, waits for them, and re-layouts, body(): mapped = owner_rows[pair_rows[0]] - owner_rows[pair_rows[1]]  91.1 us
    psum x1, blocking collectives, body(): norm_next = lax.psum(jnp.sum(resid_next * precond), ('group', 'pencil'))  74 us
    psum x1, blocking collectives, body(): old_norm = lax.psum(old_part, ('group', 'pencil'))  73.3 us
    psum x1, blocking collectives, body(): total_coarse = lax.psum(local_coarse, ('group', 'pencil'))  72.8 us
    unnamed x40, local copies, waits for them, and re-layouts  70.6 us
    scatter x2, local copies, waits for them, and re-layouts, body(): back_rows = jnp.zeros((rows_count,), jnp.float32).at[pair_rows[0]].set(se...  63.2 us
    scatter x1, local copies, waits for them, and re-layouts, load_slab(): jnp.zeros((cycle_total,), jnp.float32).at[positions].set(arrived_rows)  60.8 us
  transfers between devices with their start and end apart: 4, of which 4 were waited for; matrix products, arithmetic and copies ran while one was open for 0% of the time, Pallas kernels for 0%

commit v1 on v0

--- a/solution.py
+++ b/solution.py
@@ -2,6 +2,7 @@
 import jax.numpy as jnp
 from jax import lax
 from jax.sharding import PartitionSpec as P
+from jax.lax import all_to_all, psum
 
 
 def cycle_slot(index, extent):
@@ -76,12 +77,10 @@
     row_start = my_slab * slab_x
     positions = cycle_slot(cycle_cells, extent)
     partial_yz = forward_yz(load_slab(arrived_rows, positions, slab_shape), basis)
-    columns = lax.all_to_all(
-        partial_yz.reshape(slab_x, patches, components, extent * extent),
-        "pencil",
-        split_axis=3,
-        concat_axis=0,
-        tiled=True,
+    in_array = partial_yz.reshape(slab_x, patches, components, extent * extent)
+    columns = jnp.concatenate(
+        all_to_all(jnp.stack(jnp.split(in_array, psum(1, "pencil"), axis=3)), "pencil", 0, 0),
+        axis=0,
     )
     columns = columns.reshape(extent, patches, components, slab_x, extent)
     spectral = jnp.einsum("xpcjk,pxi->ipcjk", columns, basis[:, 0], precision=highest)

time: 881 us -> 762 us (0.86)
  local copies, waits for them, and re-layouts: 521 us -> 406 us
    unnamed x40 -> x45, local copies, waits for them, and re-layouts: 70.6 us -> 4.92 us
    reshape x2 -> x1, local copies, waits for them, and re-layouts: 37.2 us -> 2.42 us  [apply_inverse(): in_array = partial_yz.reshape(slab_x, patches, components, extent * extent)]
    all_to_all x2 -> x1, local copies, waits for them, and re-layouts: 21.2 us -> 1.32 us  [apply_inverse(): all_to_all(jnp.stack(jnp.split(in_array, psum(1, 'pencil'), axis=3)), 'pe...]
  transfers between devices with their start and end apart: 4 -> 4, of which waited for: 4 -> 4; matrix products, arithmetic and copies ran while one was open for 0% -> 1% of each run, Pallas kernels for 0% -> 0%
where the time goes in v1:
time: 762 us; the launch traced here: 757 us
  local copies, waits for them, and re-layouts  406 us (53%)
  blocking collectives  220 us (29%)
  waiting for transfers between devices  54.7 us (7%)
  matrix products  33.9 us (4%)
  starting transfers between devices  28.2 us (4%)
  other arithmetic  9.74 us (1%)
    gather x1, local copies, waits for them, and re-layouts, apply_inverse(): return volume_to_cycle(displace).reshape(-1)[positions]  160 us
    gather x2, local copies, waits for them, and re-layouts, body(): mapped = owner_rows[pair_rows[0]] - owner_rows[pair_rows[1]]  91.1 us
    psum x1, blocking collectives, body(): norm_next = lax.psum(jnp.sum(resid_next * precond), ('group', 'pencil'))  74 us
    psum x1, blocking collectives, body(): old_norm = lax.psum(old_part, ('group', 'pencil'))  73.3 us
    psum x1, blocking collectives, body(): total_coarse = lax.psum(local_coarse, ('group', 'pencil'))  72.8 us
    scatter x2, local copies, waits for them, and re-layouts, body(): back_rows = jnp.zeros((rows_count,), jnp.float32).at[pair_rows[0]].set(se...  63.1 us
    scatter x1, local copies, waits for them, and re-layouts, load_slab(): jnp.zeros((cycle_total,), jnp.float32).at[positions].set(arrived_rows)  60.9 us
    all_to_all x1, waiting for transfers between devices, apply_inverse(): lax.all_to_all(mixed, 'pencil', split_axis=0, concat_axis=3, tiled=True)  19.3 us
  transfers between devices with their start and end apart: 4, of which 4 were waited for; matrix products, arithmetic and copies ran while one was open for 1% of the time, Pallas kernels for 0%

profile of v1, /device:TPU:1, one launch (start us, length us, event | category | flops | bytes accessed | tf_op | source)
XLA Modules:
  0.0 757.2 jit_solution(11894205898412323725)
XLA Ops:
  0.6 1.0 compare_select_fusion.4
  1.7 0.8 neg.3
  2.4 31.2 %scatter_custom_fusion = f32[16384]{0:T(1024)} fusion(s32[8192]{0:T(1024)S(1)} %bitcast.191, f32[8192]{0:T(1024)} %bitcast.181, f32[]{:T(128)} %constant.16.clone.1), kind=kCustom, calls=%fused_computation.97 | custom fusion | bytes 66048 | tf_op jit(solution)/shard_map/scatter | solution.py:130
  33.7 31.9 %scatter_fusion = f32[16384]{0:T(1024)} fusion(f32[16384]{0:T(1024)} %scatter_custom_fusion, s32[8192]{0:T(1024)S(1)} %bitcast.178, f32[8192]{0:T(1024)S(1)} %neg.3), kind=kCustom, calls=%fused_computation.5 | custom fusion | bytes 131072 | tf_op jit(solution)/shard_map/scatter | solution.py:132
  65.6 12.0 %all-to-all-start = ((f32[32,1,512]{2,1,0:T(1,128)}), f32[32,1,512]{2,1,0:T(1,128)S(1)}, u32[]{:S(2)}, u32[]{:S(2)}) async-start(f32[32,1,512]{2,1,0:T(1,128)} %bitcast.11), calls=%async_computation | async-start | bytes 131072 | tf_op jit(solution)/shard_map/all_to_all | solution.py:134
  77.6 0.8 compare_select_fusion
  78.4 8.0 %all-to-all-done = f32[32,1,512]{2,1,0:T(1,128)S(1)} async-done(((f32[32,1,512]{2,1,0:T(1,128)}), f32[32,1,512]{2,1,0:T(1,128)S(1)}, u32[]{:S(2)}, u32[]{:S(2)}) %all-to-all-start) | async-done | bytes 65568 | tf_op jit(solution)/shard_map/all_to_all | solution.py:134
  86.5 60.9 %scatter_custom_fusion.2 = f32[24576]{0:T(1024)S(1)} fusion(s32[16384]{0:T(1024)S(1)} %bitcast.187, f32[16384]{0:T(1024)S(1)} %bitcast.194, f32[]{:T(128)} %constant.16.clone.1), kind=kCustom, calls=%fused_computation.88 | custom fusion | bytes 98308 | tf_op jit(solution)/shard_map/scatter | solution.py:63
  147.4 0.1 reshape_reshape.9
  147.5 0.1 fusion.67
  147.8 4.0 fusion.8
  151.9 5.2 fusion.16
  157.1 2.3 copy.108
  159.4 2.4 reshape.300
  161.8 0.7 fusion.40
  162.5 0.7 fusion.39
  163.2 0.7 fusion.38
  163.9 0.7 fusion.37
  164.6 0.7 fusion.36
  165.3 0.7 fusion.35
  166.0 0.7 fusion.34
  166.7 0.7 fusion.33
  167.4 6.6 all-to-all-start.1
  174.1 0.1 copy.113
  174.2 0.1 copy.112
  174.3 0.1 copy.114
  174.7 0.7 broadcast_add_fusion
  175.4 19.1 %all-to-all-done.1 = f32[8,8,4,3,512]{4,1,3,2,0:T(8,128)S(1)} async-done(((f32[8,8,4,3,512]{4,1,3,2,0:T(8,128)}), f32[8,8,4,3,512]{4,1,3,2,0:T(8,128)S(1)}, u32[]{:S(2)}, u32[]{:S(2)}) %all-to-all-start.1) | async-done | bytes 1572896 | tf_op jit(solution)/shard_map/all_to_all | solution.py:82
  194.5 1.3 copy.109
  195.8 2.4 reshape_reshape.10
  198.3 5.1 fusion.5
  203.4 3.2 fusion.2
  206.7 2.1 copy.115
  208.7 4.6 all-to-all-start.2
  213.3 0.6 broadcast_clamp_fusion.1
  214.0 0.6 broadcast_clamp_fusion
  214.6 19.3 %all-to-all-done.2 = f32[64,4,3,512]{3,1,2,0:T(4,128)S(1)} async-done(((f32[64,4,3,512]{3,1,2,0:T(4,128)}), f32[64,4,3,512]{3,1,2,0:T(4,128)S(1)}, u32[]{:S(2)}, u32[]{:S(2)}) %all-to-all-start.2) | async-done | bytes 1572896 | tf_op jit(solution)/shard_map/all_to_all | solution.py:91
  233.9 0.5 copy.144
  234.4 2.1 copy.132
  236.5 2.6 reshape.377
  239.2 5.1 fusion.43
  244.3 5.1 fusion.19
  249.4 2.7 fusion.66
  252.3 2.5 copy.120
  254.8 1.5 copy.121
  256.4 0.2 pad_maximum_fusion
  256.7 0.1 reshape_reshape.11
  256.8 160.3 %gather_fusion = f32[16384]{0:T(1024)} fusion(f32[24576]{0:T(1024)S(1)} %reshape_reshape.11, s32[16384]{0:T(1024)S(1)} %copy-done.8), kind=kCustom, calls=%fused_computation | custom fusion | bytes 196608 | tf_op jit(solution)/shard_map/gather | solution.py:95
  417.1 1.6 gather_fusion.1
  418.7 0.2 fusion.48
  418.9 72.8 %psum.29 = f32[1024]{0:T(1024)S(1)} all-reduce(f32[1024]{0:T(1024)S(1)} %bitcast.199), channel_id=1, replica_groups=mesh['group'=32,'pencil'=8] {'group','pencil'}, use_global_device_ids=true, to_apply=%region_5.6 | all-reduce | flops 1024 | bytes 8192 | tf_op jit(solution)/shard_map/psum | solution.py:142
  491.7 5.6 convolution_bitcast_fusion
  497.3 0.2 convolution_bitcast_fusion.1
  497.5 2.2 scatter_fusion.1
  499.8 5.0 all-to-all-start.3
  504.8 0.6 fusion.59
  505.4 8.2 %all-to-all-done.3 = f32[32,1,512]{2,1,0:T(1,128)S(1)} async-done(((f32[32,1,512]{2,1,0:T(1,128)}), f32[32,1,512]{2,1,0:T(1,128)S(1)}, u32[]{:S(2)}, u32[]{:S(2)}) %all-to-all-start.3) | async-done | bytes 65568 | tf_op jit(solution)/shard_map/all_to_all | solution.py:145
  513.7 45.5 %gather_fusion.3 = f32[8192]{0:T(1024)S(1)} fusion(f32[16384]{0:T(1024)S(1)} %bitcast.174, s32[8192]{0:T(1024)S(1)} %copy-done.11), kind=kCustom, calls=%fused_computation.3 | custom fusion | bytes 98304 | tf_op jit(solution)/shard_map/gather | solution.py:148
  559.2 45.5 %gather_fusion.2 = f32[8192]{0:T(1024)S(1)} fusion(f32[16384]{0:T(1024)S(1)} %bitcast.175, s32[8192]{0:T(1024)S(1)} %broadcast_clamp_fusion.2), kind=kCustom, calls=%fused_computation.2 | custom fusion | bytes 98304 | tf_op jit(solution)/shard_map/gather | solution.py:148
  604.8 0.6 multiply_reduce_fusion
  605.4 73.3 %all-reduce = (f32[]{:T(128)}, f32[]{:T(128)}) all-reduce(f32[]{:T(128)} %fusion.59, f32[]{:T(128)} %get-tuple-element.9), channel_id=1, replica_groups=mesh['group'=32,'pencil'=8] {'group','pencil'}, use_global_device_ids=true, to_apply=%region_1.0 | all-reduce | flops 2 | bytes 16 | tf_op jit(solution)/shard_map/psum | solution.py:126
  680.0 0.6 fusion.60
  680.6 74.0 %psum.31 = f32[]{:T(128)} all-reduce(f32[]{:T(128)} %get-tuple-element.7), channel_id=1, replica_groups=mesh['group'=32,'pencil'=8] {'group','pencil'}, use_global_device_ids=true, to_apply=%region_10.11 | all-reduce | flops 1 | bytes 8 | tf_op jit(solution)/shard_map/psum | solution.py:154
  756.0 0.7 multiply_add_fusion
  (58 shorter events, 0.8 us)
Async XLA Ops:
  1.6 64.0 %copy-start.1 = (s32[8192,1]{0,1:T(1,128)}, s32[8192,1]{0,1:T(1,128)S(1)}, u32[]{:S(2)}) copy-start(s32[8192,1]{0,1:T(1,128)S(1)} %get-tuple-element.19) | copy-start | bytes 98308
  1.6 63.9 %copy-start.9 = (s32[8192,1]{0,1:T(1,128)}, s32[8192,1]{0,1:T(1,128)S(1)}, u32[]{:S(2)}) copy-start(s32[8192,1]{0,1:T(1,128)S(1)} %get-tuple-element.20) | copy-start | bytes 98308
  33.7 44.0 %copy-start.12 = (s32[1,1,16384]{2,1,0:T(1,128)S(1)}, s32[1,1,16384]{2,1,0:T(1,128)}, u32[]{:S(2)}) copy-start(s32[1,1,16384]{2,1,0:T(1,128)} %param.20) | copy-start | bytes 196612
  33.7 114.2 %copy-start = (f32[4,3,64,64]{3,2,1,0:T(8,128)S(1)}, f32[4,3,64,64]{3,2,1,0:T(8,128)}, u32[]{:S(2)}) copy-start(f32[4,3,64,64]{3,2,1,0:T(8,128)} %param.16) | copy-start | bytes 589828
  65.6 20.9 %all-to-all-start = ((f32[32,1,512]{2,1,0:T(1,128)}), f32[32,1,512]{2,1,0:T(1,128)S(1)}, u32[]{:S(2)}, u32[]{:S(2)}) async-start(f32[32,1,512]{2,1,0:T(1,128)} %bitcast.11), calls=%async_computation | async-start | bytes 131072 | tf_op jit(solution)/shard_map/all_to_all | solution.py:134
  78.4 8.1 %copy-start.6 = (s32[16384,1]{0,1:T(1,128)}, s32[16384,1]{0,1:T(1,128)S(1)}, u32[]{:S(2)}) copy-start(s32[16384,1]{0,1:T(1,128)S(1)} %compare_select_fusion) | copy-start | bytes 196612
  161.8 12.2 %copy-start.13 = (f32[4,3,3]{2,0,1:T(4,128)S(1)}, f32[4,3,3]{2,0,1:T(4,128)}, u32[]{:S(2)}) copy-start(f32[4,3,3]{2,0,1:T(4,128)} %param.18) | copy-start | bytes 436
  161.8 12.6 %copy-start.16 = (f32[4,3,64]{2,0,1:T(4,128)S(1)}, f32[4,3,64]{2,0,1:T(4,128)}, u32[]{:S(2)}) copy-start(f32[4,3,64]{2,0,1:T(4,128)} %param.17) | copy-start | bytes 9220
  167.4 27.2 %all-to-all-start.1 = ((f32[8,8,4,3,512]{4,1,3,2,0:T(8,128)}), f32[8,8,4,3,512]{4,1,3,2,0:T(8,128)S(1)}, u32[]{:S(2)}, u32[]{:S(2)}) async-start(f32[8,8,4,3,512]{4,1,3,2,0:T(8,128)} %fusion.33), calls=%async_computation.1 | async-start | bytes 3145728 | tf_op jit(solution)/shard_map/all_to_all | solution.py:82
  198.3 5.1 copy-start.14
  206.7 6.7 copy-start.17
  208.7 4.6 copy-start.2
  208.7 5.2 copy-start.7
  208.7 25.2 %all-to-all-start.2 = ((f32[64,4,3,512]{3,1,2,0:T(4,128)}), f32[64,4,3,512]{3,1,2,0:T(4,128)S(1)}, u32[]{:S(2)}, u32[]{:S(2)}) async-start(f32[64,4,3,512]{3,1,2,0:T(4,128)} %copy.115), calls=%async_computation.2 | async-start | bytes 3145728 | tf_op jit(solution)/shard_map/all_to_all | solution.py:91
  252.2 4.6 copy-start.8
  256.8 161.9 %copy-start.18 = (s32[1,1,32]{2,1,0:T(1,128)S(1)}, s32[1,1,32]{2,1,0:T(1,128)}, u32[]{:S(2)}) copy-start(s32[1,1,32]{2,1,0:T(1,128)} %param.23) | copy-start | bytes 388
  417.1 87.7 %copy-start.10 = (s32[8192,1]{0,1:T(1,128)S(1)}, s32[8192,1]{0,1:T(1,128)}, u32[]{:S(2)}) copy-start(s32[8192,1]{0,1:T(1,128)} %copy-done.9) | copy-start | bytes 98308
  417.1 87.7 %copy-start.4 = (f32[1,1,8192]{2,1,0:T(1,128)S(1)}, f32[1,1,8192]{2,1,0:T(1,128)}, u32[]{:S(2)}) copy-start(f32[1,1,8192]{2,1,0:T(1,128)} %param.15) | copy-start | bytes 98308
  417.1 87.7 %copy-start.5 = (f32[1,1,8192]{2,1,0:T(1,128)S(1)}, f32[1,1,8192]{2,1,0:T(1,128)}, u32[]{:S(2)}) copy-start(f32[1,1,8192]{2,1,0:T(1,128)} %param.13) | copy-start | bytes 98308
  417.1 96.6 %copy-start.11 = (s32[8192]{0:T(1024)S(1)}, s32[8192]{0:T(1024)}, u32[]{:S(2)}) copy-start(s32[8192]{0:T(1024)} %broadcast_clamp_fusion.1) | copy-start | bytes 98308
  499.8 13.9 %all-to-all-start.3 = ((f32[32,1,512]{2,1,0:T(1,128)}), f32[32,1,512]{2,1,0:T(1,128)S(1)}, u32[]{:S(2)}, u32[]{:S(2)}) async-start(f32[32,1,512]{2,1,0:T(1,128)} %bitcast.61), calls=%async_computation.3 | async-start | bytes 131072 | tf_op jit(solution)/shard_map/all_to_all | solution.py:145
  559.2 45.6 %copy-start.3 = (f32[1,1,8192]{2,1,0:T(1,128)S(1)}, f32[1,1,8192]{2,1,0:T(1,128)}, u32[]{:S(2)}) copy-start(f32[1,1,8192]{2,1,0:T(1,128)} %param.14) | copy-start | bytes 98308
  559.2 196.8 %copy-start.15 = (f32[1,1,8192]{2,1,0:T(1,128)S(1)}, f32[1,1,8192]{2,1,0:T(1,128)}, u32[]{:S(2)}) copy-start(f32[1,1,8192]{2,1,0:T(1,128)} %param.12) | copy-start | bytes 98308
